TPU v7x, 32 devices: a whole 2x2x4 slice. The times are simulated.
32 devices in a mesh: group: 1, path: 32 (over z, y, x, core).
Axes of the slice: x: 2, y: 2, z: 4, core: 2. Of those that a mesh axis runs over, the one named last changes fastest.
Arguments:
- normals: float32 [8, 32, 8192], P(None, None, ('group', 'path')), may hold values from -6 to 6
- start_state: float32 [32, 8192], P(None, ('group', 'path')), may hold values from -0.12 to 0.12
- later_adjoint: float32 [32, 8192], P(None, ('group', 'path')), may hold values from -1.8 to 1.8
- vol: float32 [8], replicated, may hold values from 0.004 to 0.016
- factor_load: float32 [32, 960], replicated, may hold values from -2.1 to 2.1
- knots: float32 [960], replicated, may hold values from 0.01 to 0.05
- spline_jac: float32 [960, 960], replicated
- cashflows: bfloat16 [256, 960], P(('group', 'path')), may hold values from -0.1875 to 0.1875
- trade_set: int32 [256, 1], P(('group', 'path')), may hold values from 0 to 127
- trade_end: int32 [256], P(('group', 'path')), may hold values from 240 to 960
- set_cpty: int32 [128, 1], P('group'), may hold values from 0 to 63
- default_prob: float32 [8, 64], replicated, may hold values from 0.01 to 0.1
- base_value: float32 [8, 128], P(None, 'group'), may hold values from -3 to 3
Outputs:
- knot_grad: float32 [960], P('group')
- alloc: float32 [256], P(('group', 'path'))
- start_adjoint: float32 [32, 8192], P(None, ('group', 'path'))
All inputs are finite; a program needn't handle non-finite values.
Results may differ from a plain program's by a relative error of at most 0.0011.
Values may be sent and summed in bfloat16 or wider, within the bound.
No kernel may reach another device: no remote copies, remote signals or barrier semaphores. Data moves between devices by JAX's collectives and lax.ppermute only.
A program may use at most 64 MiB of HBM per device.

v0:
```python
import math
import jax
import jax.numpy as jnp
from jax import lax
from jax.sharding import PartitionSpec as P

MEAN_REV = 0.05
STEP_YEARS = 0.25
HORIZON_YEARS = 30.0
SHARPNESS = 4.0
LOSS_RATE = 0.6


def curve_terms(knots, spline_jac, date_count, knot_count):
    zero_rate = jnp.dot(spline_jac, knots, precision=lax.Precision.HIGHEST)
    knot_index = jnp.arange(knot_count, dtype=jnp.int32)
    date_index = jnp.arange(date_count, dtype=jnp.int32)
    is_alive = 120 * (knot_index[None, :] + 1) > knot_count * (date_index[:, None] + 1)
    maturity = HORIZON_YEARS * (knot_index + 1).astype(jnp.float32) / knot_count
    fixing = STEP_YEARS * (date_index + 1).astype(jnp.float32)
    horizon = jnp.where(is_alive, maturity[None, :] - fixing[:, None], jnp.float32(0.0))
    loading = (1.0 - jnp.exp(-MEAN_REV * horizon)) / MEAN_REV
    discount = jnp.where(is_alive, jnp.exp(-zero_rate[None, :] * horizon), jnp.float32(0.0))
    return (horizon, loading, discount)


def state_path(start_state, vol, normals):
    decay_factor = math.exp(-MEAN_REV * STEP_YEARS)
    state = start_state
    collected = []
    for index in range(normals.shape[0]):
        state = decay_factor * state + vol[index] * normals[index]
        collected.append(state)
    return jnp.stack(collected)


def per_device(
    normals,
    start_state,
    later_adjoint,
    vol,
    factor_load,
    knots,
    spline_jac,
    cashflows,
    trade_set,
    trade_end,
    set_cpty,
    default_prob,
    base_value,
):
    highest = lax.Precision.HIGHEST
    date_count = normals.shape[0]
    knot_count = knots.shape[0]
    set_count = base_value.shape[1]
    paths_all = normals.shape[2] * lax.axis_size("path")
    horizon, loading, discount = curve_terms(knots, spline_jac, date_count, knot_count)
    knot_index = jnp.arange(knot_count, dtype=jnp.int32)
    live_flows = jnp.where(
        knot_index[None, :] < trade_end[:, None], cashflows, jnp.zeros_like(cashflows)
    )
    set_ids = trade_set[:, 0]
    labels = jnp.arange(set_count, dtype=jnp.int32)
    all_flows, all_sets = (
        lax.all_gather(live_flows, "path", axis=0, tiled=True),
        lax.all_gather(set_ids, "path", axis=0, tiled=True),
    )
    member = (labels[:, None] == all_sets[None, :]).astype(jnp.bfloat16)
    net_flows = jnp.dot(member, all_flows, preferred_element_type=jnp.float32).astype(jnp.bfloat16)
    counter = (
        jnp.arange(default_prob.shape[1], dtype=jnp.int32)[:, None] == set_cpty[:, 0][None, :]
    ).astype(jnp.float32)
    weight = LOSS_RATE * jnp.dot(default_prob, counter, precision=highest)
    states = state_path(start_state, vol, normals)
    shift = jnp.einsum("fm,ifp->imp", factor_load, states, precision=highest)
    bond_term = jnp.exp(-loading[:, :, None] * shift)
    feat_exact = discount[:, :, None] * bond_term
    features = feat_exact.astype(jnp.bfloat16)
    values = jnp.einsum("nm,imp->inp", net_flows, features, preferred_element_type=jnp.float32)
    mean_value = lax.psum(jnp.sum(values, axis=2), "path") / paths_all
    shifted = values - mean_value[:, :, None] + base_value[:, :, None]
    slope = weight[:, :, None] * jax.nn.sigmoid(SHARPNESS * shifted)
    mean_slope = lax.psum(jnp.sum(slope, axis=2), "path") / paths_all
    set_adjoint = (slope - mean_slope[:, :, None]).astype(jnp.bfloat16)
    feat_adjoint = jnp.einsum(
        "nm,inp->imp", net_flows, set_adjoint, preferred_element_type=jnp.float32
    )
    state_local = -jnp.einsum(
        "fm,imp->ifp",
        factor_load,
        feat_adjoint * feat_exact * loading[:, :, None],
        precision=highest,
    )
    discount_grad = jnp.sum(feat_adjoint * bond_term, axis=2)
    rate_adjoint = -jnp.sum(discount_grad * discount * horizon, axis=0) / paths_all
    rate_total = lax.psum(rate_adjoint, "path")
    knot_grad = jnp.dot(spline_jac.T, rate_total, precision=highest)
    load_sums = (
        jnp.einsum("inp,imp->nm", set_adjoint, features, preferred_element_type=jnp.float32)
        / paths_all
    )
    set_rows = load_sums[all_sets]
    trade_part = jnp.sum(all_flows.astype(jnp.float32) * set_rows, axis=1)
    alloc = lax.psum_scatter(trade_part, "path", scatter_dimension=0, tiled=True)
    decay_factor = math.exp(-MEAN_REV * STEP_YEARS)
    carried = later_adjoint + state_local[date_count - 1]
    for index in reversed(range(date_count - 1)):
        carried = state_local[index] + decay_factor * carried
    start_adjoint = decay_factor * carried
    return (knot_grad, alloc, start_adjoint)


def solution(mesh):
    in_specs = (
        P(None, None, ("group", "path")),
        P(None, ("group", "path")),
        P(None, ("group", "path")),
        P(),
        P(),
        P(),
        P(),
        P(("group", "path"), None),
        P(("group", "path"), None),
        P(("group", "path")),
        P("group", None),
        P(),
        P(None, "group"),
    )
    out_specs = (P("group"), P(("group", "path")), P(None, ("group", "path")))
    return jax.shard_map(
        per_device, mesh=mesh, in_specs=in_specs, out_specs=out_specs, check_vma=False
    )
```

profile of v0, /device:TPU:0, one launch (start us, length us, event | category | flops | bytes accessed | tf_op | source)
XLA Modules:
  0.0 270.6 jit_solution(15762425865365894682)
XLA Ops:
  0.7 0.8 bitcast_dynamic-update-slice_fusion.8
  1.5 41.9 %all-reduce = s32[256]{0:T(256)S(1)} all-reduce(s32[256]{0:T(256)S(1)} %bitcast_dynamic-update-slice_fusion.8), channel_id=2, replica_groups=mesh['group'=1,'path'=32] {'path'}, use_global_device_ids=true, to_apply=%add | all-reduce | flops 256 | bytes 2048 | tf_op jit(solution)/shard_map/all_gather | solution.py:66
  43.4 0.6 pad_clamp_fusion
  44.0 0.8 fusion.18
  44.9 5.4 %fusion.50 = f32[1,960]{1,0:T(1,128)S(1)} fusion(f32[960,960]{1,0:T(8,128)} %param.19, f32[960,1]{0,1:T(1,128)} %bitcast.192), kind=kOutput, calls=%fused_computation.96 | convolution fusion | flops 11059200 | bytes 3694080 | tf_op jit(solution)/shard_map/dot_general | solution.py:15
  50.3 1.6 fusion.48
  52.0 0.8 fusion.42
  52.8 0.7 subtract_multiply_fusion
  53.5 1.5 bitcast_dynamic-update-slice_fusion.7
  54.9 2.0 bitcast_dynamic-update-slice_fusion.6
  57.0 1.5 bitcast_dynamic-update-slice_fusion.5
  58.4 2.0 bitcast_dynamic-update-slice_fusion.4
  60.5 1.5 bitcast_dynamic-update-slice_fusion.3
  61.9 2.1 bitcast_dynamic-update-slice_fusion.2
  64.1 1.4 bitcast_dynamic-update-slice_fusion.1
  65.4 2.1 bitcast_dynamic-update-slice_fusion
  67.5 41.7 %all_gather.7 = bf16[256,960]{1,0:T(8,128)(2,1)S(1)} all-gather(bf16[8,960]{1,0:T(8,128)(2,1)S(1)} %fusion.42), channel_id=1, replica_groups=mesh['group'=1,'path'=32] {'path'}, dimensions={0}, use_global_device_ids=true | all-gather | bytes 506880 | tf_op jit(solution)/shard_map/all_gather | solution.py:65
  109.2 0.3 fusion.17
  109.6 6.5 %fusion.23 = f32[8,256,960]{1,2,0:T(8,128)S(1)} fusion(f32[8,32,256]{2,1,0:T(8,128)S(1)} %bitcast_dynamic-update-slice_fusion, f32[32,960]{1,0:T(8,128)S(1)} %copy-done), kind=kOutput, calls=%fused_computation.28 | convolution fusion | flops 754974720 | bytes 8249344 | tf_op jit(solution)/shard_map/fm,ifp->imp/dot_general | solution.py:75
  116.1 3.1 %copy-done.1 = f32[8,256,960]{1,2,0:T(8,128)} copy-done((f32[8,256,960]{1,2,0:T(8,128)}, f32[8,256,960]{1,2,0:T(8,128)S(1)}, u32[]{:S(2)}) %copy-start.1) | copy-done | bytes 7864344
  119.1 5.4 %fusion.49 = (f32[8,128]{1,0:T(8,128)S(1)}, f32[8,128,256]{1,2,0:T(8,128)S(1)}) fusion(bf16[128,960,1]{0,1,2:T(8,128)(2,1)S(1)} %fusion.17, f32[8,256,960]{1,2,0:T(8,128)S(1)} %fusion.23, f32[8,960]{1,0:T(8,128)S(1)} %get-tuple-element.12, f32[8,960]{1,0:T(8,128)S(1)} %get-tuple-element.13), kind=kOutput, calls=%fused_computation.95 | convolution fusion | flops 509475840 | bytes 9224192 | tf_op jit(solution)/shard_map/nm,imp->inp/dot_general | solution.py:79
  124.6 37.0 %psum.21 = f32[8,128]{1,0:T(8,128)S(1)} all-reduce(f32[8,128]{1,0:T(8,128)S(1)} %get-tuple-element.22), channel_id=1, replica_groups=mesh['group'=1,'path'=32] {'path'}, use_global_device_ids=true, to_apply=%region_1.2 | all-reduce | flops 1024 | bytes 8192 | tf_op jit(solution)/shard_map/psum | solution.py:80
  162.0 41.2 %psum.22 = f32[8,128]{1,0:T(8,128)S(1)} all-reduce(f32[8,128]{1,0:T(8,128)S(1)} %fusion.47), channel_id=1, replica_groups=mesh['group'=1,'path'=32] {'path'}, use_global_device_ids=true, to_apply=%region_3.4 | all-reduce | flops 1024 | bytes 8192 | tf_op jit(solution)/shard_map/psum | solution.py:83
  203.2 0.6 copy-done.15
  203.8 5.4 %fusion.10 = f32[128,960]{0,1:T(8,128)S(1)} fusion(f32[8,256,960]{1,2,0:T(8,128)} %copy-done.1, f32[8,960]{1,0:T(8,128)S(1)} %get-tuple-element.12, f32[8,960]{1,0:T(8,128)S(1)} %get-tuple-element.13, f32[8,128]{1,0:T(8,128)S(1)} %broadcast_multiply_fusion, f32[8,128,256]{1,2,0:T(8,128)S(1)} %get-tuple-element.23, f32[8,128]{1,0:T(8,128)S(1)} %copy-done.13, ...), kind=kOutput, calls=%fused_computation.16 | convolution fusion | flops 511696896 | bytes 9482240 | tf_op jit(solution)/shard_map/inp,imp->nm/dot_general | solution.py:99
  209.4 1.2 gather_fusion
  210.8 6.4 %fusion = (f32[8,960]{1,0:T(8,128)S(1)}, f32[8,256,960]{1,2,0:T(8,128)S(1)}) fusion(f32[8,256,960]{1,2,0:T(8,128)} %copy-done.1, f32[8,960]{1,0:T(8,128)S(1)} %get-tuple-element.12, bf16[128,960,1]{0,1,2:T(8,128)(2,1)S(1)} %fusion.17, f32[8,128]{1,0:T(8,128)} %copy-done.15, f32[8,128]{1,0:T(8,128)} %param.25, f32[8,128,256]{1,2,0:T(8,128)S(1)} %get-tuple-element.23, ...), kind=kOutput, calls=%fused_computation.3 | convolution fusion | flops 511566336 | bytes 17100800 | tf_op jit(solution)/shard_map/nm,inp->imp/dot_general | solution.py:85
  217.4 7.6 %fusion.14 = f32[8,32,256]{2,1,0:T(8,128)S(1)} fusion(f32[8,256,960]{1,2,0:T(8,128)S(1)} %get-tuple-element.25, f32[8,256,960]{1,2,0:T(8,128)S(1)} %bitcast.190, f32[8,960]{1,0:T(8,128)S(1)} %copy-done.4, f32[8,960]{1,0:T(8,128)S(1)} %get-tuple-element.12, f32[8,960]{1,0:T(8,128)S(1)} %copy-done.3, f32[32,960]{1,0:T(8,128)S(1)} %copy-done), kind=kOutput, calls=%fused_computation.19 | convolution fusion | flops 762904576 | bytes 16205824 | tf_op jit(solution)/shard_map/fm,imp->ifp/dot_general | solution.py:88
  225.0 0.6 fusion.41
  225.7 39.6 %all-reduce.2 = (f32[960]{0:T(1024)S(1)}, f32[256]{0:T(256)S(1)}) all-reduce(f32[960]{0:T(1024)S(1)} %negate_multiply_fusion, f32[256]{0:T(256)S(1)} %multiply_reduce_fusion), channel_id=1, replica_groups=mesh['group'=1,'path'=32] {'path'}, use_global_device_ids=true, to_apply=%region_6.7 | all-reduce | flops 1216 | bytes 9728 | tf_op jit(solution)/shard_map/psum | solution.py:96
  265.3 4.7 %fusion.5 = f32[1,960]{1,0:T(1,128)} fusion(f32[960,1]{0,1:T(1,128)S(1)} %bitcast.194, f32[960,960]{1,0:T(8,128)} %param.19), kind=kOutput, calls=%fused_computation.9 | convolution fusion | flops 11059200 | bytes 3694080 | tf_op jit(solution)/shard_map/dot_general | solution.py:97
  270.0 0.6 dynamic-slice
  (57 shorter events, 1.0 us)
Async XLA Ops:
  0.6 108.9 %copy-start = (f32[32,960]{1,0:T(8,128)S(1)}, f32[32,960]{1,0:T(8,128)}, u32[]{:S(2)}) copy-start(f32[32,960]{1,0:T(8,128)} %param.17) | copy-start | bytes 368644
  0.7 123.9 %copy-start.16 = (s32[8]{0:T(128)}, s32[8]{0:T(128)S(1)}, u32[]{:S(2)}) copy-start(s32[8]{0:T(128)S(1)} %fusion.46) | copy-start | bytes 100
  0.7 123.9 %copy-start.18 = (f32[8]{0:T(128)}, f32[8]{0:T(128)S(1)}, u32[]{:S(2)}) copy-start(f32[8]{0:T(128)S(1)} %convert_multiply_fusion.1) | copy-start | bytes 100
  44.8 158.3 %copy-start.14 = (f32[8,128]{1,0:T(8,128)}, f32[8,128]{1,0:T(8,128)S(1)}, u32[]{:S(2)}) copy-start(f32[8,128]{1,0:T(8,128)S(1)} %fusion.18) | copy-start | bytes 12292
  44.8 79.7 %copy-start.5 = (s32[960]{0:T(1024)}, s32[960]{0:T(1024)S(1)}, u32[]{:S(2)}) copy-start(s32[960]{0:T(1024)S(1)} %fusion.44) | copy-start | bytes 11524
  44.9 79.7 %copy-start.7 = (f32[960]{0:T(1024)}, f32[960]{0:T(1024)S(1)}, u32[]{:S(2)}) copy-start(f32[960]{0:T(1024)S(1)} %convert_multiply_fusion) | copy-start | bytes 11524
  50.3 74.3 %copy-start.9 = (f32[960]{0:T(1024)}, f32[960]{0:T(1024)S(1)}, u32[]{:S(2)}) copy-start(f32[960]{0:T(1024)S(1)} %neg.24) | copy-start | bytes 11524
  53.5 149.7 %copy-start.2 = (f32[8,960]{1,0:T(8,128)}, f32[8,960]{1,0:T(8,128)S(1)}, u32[]{:S(2)}) copy-start(f32[8,960]{1,0:T(8,128)S(1)} %get-tuple-element.13) | copy-start | bytes 92164
  109.6 52.1 %copy-start.13 = (f32[8,128]{1,0:T(8,128)S(1)}, f32[8,128]{1,0:T(8,128)}, u32[]{:S(2)}) copy-start(f32[8,128]{1,0:T(8,128)} %param.25) | copy-start | bytes 12292
  116.1 3.1 %copy-start.1 = (f32[8,256,960]{1,2,0:T(8,128)}, f32[8,256,960]{1,2,0:T(8,128)S(1)}, u32[]{:S(2)}) copy-start(f32[8,256,960]{1,2,0:T(8,128)S(1)} %fusion.23) | copy-start | bytes 23592964
  161.6 41.5 %copy-start.11 = (f32[8,128]{1,0:T(8,128)}, f32[8,128]{1,0:T(8,128)S(1)}, u32[]{:S(2)}) copy-start(f32[8,128]{1,0:T(8,128)S(1)} %broadcast_multiply_fusion.1) | copy-start | bytes 12292
  203.2 0.6 copy-start.15
  210.6 6.7 %slice-start = ((s8[7864320]{0:T(1024)(128)(4,1)}), s8[4194304]{0:T(1024)(128)(4,1)S(1)}, s32[]{:S(2)}) async-start(s8[7864320]{0:T(1024)(128)(4,1)} %bitcast.189), calls=%async_computation | async-start | bytes 8388608
  210.8 6.5 %slice-start.1 = ((s8[7864320]{0:T(1024)(128)(4,1)}), s8[3670016]{0:T(1024)(128)(4,1)S(1)}, s32[]{:S(2)}) async-start(s8[7864320]{0:T(1024)(128)(4,1)} %bitcast.189), calls=%async_computation.1 | async-start | bytes 7340032
  210.8 6.5 %copy-start.3 = (f32[8,960]{1,0:T(8,128)S(1)}, f32[8,960]{1,0:T(8,128)}, u32[]{:S(2)}) copy-start(f32[8,960]{1,0:T(8,128)} %copy-done.2) | copy-start | bytes 92164
  210.8 6.5 %copy-start.4 = (f32[8,960]{1,0:T(8,128)S(1)}, f32[8,960]{1,0:T(8,128)}, u32[]{:S(2)}) copy-start(f32[8,960]{1,0:T(8,128)} %get-tuple-element.11) | copy-start | bytes 92164
  217.3 7.6 %copy-start.12 = (f32[32,256]{1,0:T(8,128)S(1)}, f32[32,256]{1,0:T(8,128)}, u32[]{:S(2)}) copy-start(f32[32,256]{1,0:T(8,128)} %param.15) | copy-start | bytes 98308
  217.3 8.3 %copy-start.6 = (s32[960]{0:T(1024)S(1)}, s32[960]{0:T(1024)}, u32[]{:S(2)}) copy-start(s32[960]{0:T(1024)} %copy-done.5) | copy-start | bytes 11524
  217.3 8.3 %copy-start.8 = (f32[960]{0:T(1024)S(1)}, f32[960]{0:T(1024)}, u32[]{:S(2)}) copy-start(f32[960]{0:T(1024)} %copy-done.7) | copy-start | bytes 11524
  217.3 8.3 %copy-start.10 = (f32[960]{0:T(1024)S(1)}, f32[960]{0:T(1024)}, u32[]{:S(2)}) copy-start(f32[960]{0:T(1024)} %copy-done.9) | copy-start | bytes 11524
  217.3 8.3 %copy-start.17 = (s32[8]{0:T(128)S(1)}, s32[8]{0:T(128)}, u32[]{:S(2)}) copy-start(s32[8]{0:T(128)} %copy-done.16) | copy-start | bytes 100
  217.4 8.3 %copy-start.19 = (f32[8]{0:T(128)S(1)}, f32[8]{0:T(128)}, u32[]{:S(2)}) copy-start(f32[8]{0:T(128)} %copy-done.18) | copy-start | bytes 100
where the time goes:
time: 272 us; the launch traced here: 271 us
  blocking collectives  201 us (74%)
  matrix products  42.6 us (16%)
  other arithmetic  17.4 us (6%)
  local copies, waits for them, and re-layouts  8.13 us (3%)
    all_gather x1, blocking collectives, per_device(): lax.all_gather(set_ids, 'path', axis=0, tiled=True)  41.9 us
    all_gather x1, blocking collectives, per_device(): lax.all_gather(live_flows, 'path', axis=0, tiled=True)  41.7 us
    psum x1, blocking collectives, per_device(): mean_slope = lax.psum(jnp.sum(slope, axis=2), 'path') / paths_all  41.2 us
    psum x1, blocking collectives, per_device(): rate_total = lax.psum(rate_adjoint, 'path')  39.6 us
    psum x1, blocking collectives, per_device(): mean_value = lax.psum(jnp.sum(values, axis=2), 'path') / paths_all  37 us
    unnamed x8, other arithmetic  12 us
    dot_general x1, matrix products, per_device(): jnp.einsum('fm,imp->ifp', factor_load, feat_adjoint * feat_exact * loadin...  7.57 us
    dot_general x1, matrix products, per_device(): shift = jnp.einsum('fm,ifp->imp', factor_load, states, precision=highest)  6.46 us

commit v1 on v0

--- a/solution.py
+++ b/solution.py
@@ -93,7 +93,8 @@
     )
     discount_grad = jnp.sum(feat_adjoint * bond_term, axis=2)
     rate_adjoint = -jnp.sum(discount_grad * discount * horizon, axis=0) / paths_all
-    rate_total = lax.psum(rate_adjoint, "path")
+    terms = lax.all_gather(rate_adjoint, "path", axis=0, tiled=False)
+    rate_total = terms.sum(axis=0)
     knot_grad = jnp.dot(spline_jac.T, rate_total, precision=highest)
     load_sums = (
         jnp.einsum("inp,imp->nm", set_adjoint, features, preferred_element_type=jnp.float32)

time: 272 us -> 353 us (1.30)
  waiting for transfers between devices: 0 us -> 64.9 us
  between operations: 1.04 us -> 14.3 us
    unnamed x0 -> x2, waiting for transfers between devices: none -> 64.9 us
    unnamed x0 -> x1, blocking collectives: none -> 39.6 us
    psum x1 -> x0, blocking collectives: 39.6 us -> none  [per_device(): rate_total = lax.psum(rate_adjoint, 'path')]
  transfers between devices with their start and end apart: 0 -> 1, of which waited for: 0 -> 1; matrix products, arithmetic and copies ran while one was open for 0% -> 5% of each run, Pallas kernels for 0% -> 0%
where the time goes in v1:
time: 353 us; the launch traced here: 352 us
  blocking collectives  201 us (57%)
  waiting for transfers between devices  64.9 us (18%)
  matrix products  46 us (13%)
  other arithmetic  16.1 us (5%)
  between operations  14.3 us (4%)
  local copies, waits for them, and re-layouts  8.9 us (3%)
    unnamed x2, waiting for transfers between devices  64.9 us
    all_gather x1, blocking collectives, per_device(): lax.all_gather(set_ids, 'path', axis=0, tiled=True)  42 us
    all_gather x1, blocking collectives, per_device(): lax.all_gather(live_flows, 'path', axis=0, tiled=True)  41.7 us
    psum x1, blocking collectives, per_device(): mean_slope = lax.psum(jnp.sum(slope, axis=2), 'path') / paths_all  41.2 us
    unnamed x1, blocking collectives  39.6 us
    psum x1, blocking collectives, per_device(): mean_value = lax.psum(jnp.sum(values, axis=2), 'path') / paths_all  37.1 us
    unnamed x8, other arithmetic  11.8 us
    dot_general x1, matrix products, per_device(): jnp.einsum('fm,imp->ifp', factor_load, feat_adjoint * feat_exact * loadin...  11.1 us
  transfers between devices with their start and end apart: 1, of which 1 were waited for; matrix products, arithmetic and copies ran while one was open for 5% of the time, Pallas kernels for 0%

profile of v1, /device:TPU:0, one launch (start us, length us, event | category | flops | bytes accessed | tf_op | source)
XLA Modules:
  0.0 351.6 jit_solution(9350441267751391414)
XLA Ops:
  7.3 0.8 bitcast_dynamic-update-slice_fusion.8
  8.0 42.0 %all-reduce = s32[256]{0:T(256)S(1)} all-reduce(s32[256]{0:T(256)S(1)} %bitcast_dynamic-update-slice_fusion.8), channel_id=2, replica_groups=mesh['group'=1,'path'=32] {'path'}, use_global_device_ids=true, to_apply=%add | all-reduce | flops 256 | bytes 2048 | tf_op jit(solution)/shard_map/all_gather | solution.py:66
  50.0 5.4 %fusion.50 = f32[1,960]{1,0:T(1,128)S(1)} fusion(f32[960,960]{1,0:T(8,128)} %param.19, f32[960,1]{0,1:T(1,128)} %bitcast.191), kind=kOutput, calls=%fused_computation.96 | convolution fusion | flops 11059200 | bytes 3694080 | tf_op jit(solution)/shard_map/dot_general | solution.py:15
  55.4 1.6 fusion.48
  57.1 0.8 fusion.42
  57.9 41.7 %all_gather.11 = bf16[256,960]{1,0:T(8,128)(2,1)S(1)} all-gather(bf16[8,960]{1,0:T(8,128)(2,1)S(1)} %fusion.42), channel_id=1, replica_groups=mesh['group'=1,'path'=32] {'path'}, dimensions={0}, use_global_device_ids=true | all-gather | bytes 506880 | tf_op jit(solution)/shard_map/all_gather | solution.py:65
  99.6 1.4 bitcast_dynamic-update-slice_fusion.7
  101.0 2.1 bitcast_dynamic-update-slice_fusion.6
  103.0 1.3 bitcast_dynamic-update-slice_fusion.5
  104.4 2.0 bitcast_dynamic-update-slice_fusion.4
  106.4 1.4 bitcast_dynamic-update-slice_fusion.3
  107.8 2.1 bitcast_dynamic-update-slice_fusion.2
  109.9 1.4 bitcast_dynamic-update-slice_fusion.1
  111.3 2.0 bitcast_dynamic-update-slice_fusion
  113.3 0.3 fusion.17
  113.7 6.5 %fusion.23 = f32[8,256,960]{1,2,0:T(8,128)S(1)} fusion(f32[8,32,256]{2,1,0:T(8,128)S(1)} %bitcast_dynamic-update-slice_fusion, f32[32,960]{1,0:T(8,128)S(1)} %copy-done), kind=kOutput, calls=%fused_computation.28 | convolution fusion | flops 754974720 | bytes 8249344 | tf_op jit(solution)/shard_map/fm,ifp->imp/dot_general | solution.py:75
  120.3 3.0 copy-done.1
  123.3 5.4 %fusion.49 = (f32[8,128]{1,0:T(8,128)S(1)}, f32[8,128,256]{1,2,0:T(8,128)S(1)}) fusion(bf16[128,960,1]{0,1,2:T(8,128)(2,1)S(1)} %fusion.17, f32[8,256,960]{1,2,0:T(8,128)S(1)} %fusion.23, f32[8,960]{1,0:T(8,128)S(1)} %get-tuple-element.10, f32[8,960]{1,0:T(8,128)S(1)} %get-tuple-element.11), kind=kOutput, calls=%fused_computation.95 | convolution fusion | flops 509475840 | bytes 9224192 | tf_op jit(solution)/shard_map/nm,imp->inp/dot_general | solution.py:79
  128.7 37.1 %psum.14 = f32[8,128]{1,0:T(8,128)S(1)} all-reduce(f32[8,128]{1,0:T(8,128)S(1)} %get-tuple-element.20), channel_id=1, replica_groups=mesh['group'=1,'path'=32] {'path'}, use_global_device_ids=true, to_apply=%region_1.2 | all-reduce | flops 1024 | bytes 8192 | tf_op jit(solution)/shard_map/psum | solution.py:80
  165.9 0.3 fusion.47
  166.2 41.2 %psum.15 = f32[8,128]{1,0:T(8,128)S(1)} all-reduce(f32[8,128]{1,0:T(8,128)S(1)} %fusion.47), channel_id=1, replica_groups=mesh['group'=1,'path'=32] {'path'}, use_global_device_ids=true, to_apply=%region_3.4 | all-reduce | flops 1024 | bytes 8192 | tf_op jit(solution)/shard_map/psum | solution.py:83
  207.4 7.0 %fusion = (f32[8,960]{1,0:T(8,128)S(1)}, f32[8,256,960]{1,2,0:T(8,128)}) fusion(f32[8,256,960]{1,2,0:T(8,128)} %copy-done.1, f32[8,960]{1,0:T(8,128)S(1)} %get-tuple-element.10, bf16[128,960,1]{0,1,2:T(8,128)(2,1)S(1)} %fusion.17, f32[8,128]{1,0:T(8,128)S(1)} %broadcast_multiply_fusion, f32[8,128]{1,0:T(8,128)S(1)} %copy-done.4, ...), kind=kOutput, calls=%fused_computation.3 | convolution fusion | flops 511566336 | bytes 17100800 | tf_op jit(solution)/shard_map/nm,inp->imp/dot_general | solution.py:85
  214.7 0.6 copy-done.2
  215.4 5.4 %fusion.10 = f32[128,960]{0,1:T(8,128)S(1)} fusion(f32[8,256,960]{1,2,0:T(8,128)} %copy-done.1, f32[8,960]{1,0:T(8,128)S(1)} %get-tuple-element.10, f32[8,960]{1,0:T(8,128)S(1)} %get-tuple-element.11, f32[8,128]{1,0:T(8,128)S(1)} %broadcast_multiply_fusion, f32[8,128,256]{1,2,0:T(8,128)S(1)} %get-tuple-element.21, f32[8,128]{1,0:T(8,128)S(1)} %copy-done.4, ...), kind=kOutput, calls=%fused_computation.16 | convolution fusion | flops 511696896 | bytes 9482240 | tf_op jit(solution)/shard_map/inp,imp->nm/dot_general | solution.py:100
  221.0 1.1 gather_fusion
  222.1 11.1 %fusion.14 = f32[8,32,256]{2,1,0:T(8,128)S(1)} fusion(f32[8,256,960]{1,2,0:T(8,128)} %get-tuple-element.23, f32[8,256,960]{1,2,0:T(8,128)} %copy-done.1, f32[8,960]{1,0:T(8,128)S(1)} %get-tuple-element.9, f32[8,960]{1,0:T(8,128)S(1)} %get-tuple-element.10, f32[8,960]{1,0:T(8,128)S(1)} %get-tuple-element.11, f32[32,960]{1,0:T(8,128)S(1)} %copy-done), kind=kOutput, calls=%fused_computation.19 | convolution fusion | flops 762904576 | bytes 16205824 | tf_op jit(solution)/shard_map/fm,imp->ifp/dot_general | solution.py:88
  233.2 0.6 fusion.41
  234.0 39.6 %all-reduce.2 = f32[256]{0:T(256)S(1)} all-reduce(f32[256]{0:T(256)S(1)} %multiply_reduce_fusion), channel_id=4, replica_groups=mesh['group'=1,'path'=32] {'path'}, use_global_device_ids=true, to_apply=%region_8.9.clone | all-reduce | flops 256 | bytes 2048
  273.6 0.6 dynamic-slice
  274.2 64.8 %all-reduce.5.cloned.1.call-done = f32[30720]{0:T(1024)} async-done(((f32[30720]{0:T(1024)}), f32[30720]{0:T(1024)}) %all-reduce.5.cloned.1.call-update) | async-done | bytes 122896
  339.0 1.0 reshape.253
  340.0 4.7 %fusion.5 = f32[1,960]{1,0:T(1,128)} fusion(f32[960,1]{0,1:T(1,128)S(1)} %bitcast.189, f32[960,960]{1,0:T(8,128)} %param.19), kind=kOutput, calls=%fused_computation.9 | convolution fusion | flops 11059200 | bytes 3694080 | tf_op jit(solution)/shard_map/dot_general | solution.py:98
  (32 shorter events, 1.0 us)
Async XLA Ops:
  7.2 106.5 %copy-start = (f32[32,960]{1,0:T(8,128)S(1)}, f32[32,960]{1,0:T(8,128)}, u32[]{:S(2)}) copy-start(f32[32,960]{1,0:T(8,128)} %param.17) | copy-start | bytes 368644
  7.2 331.9 %all-reduce.5.cloned.1.call-start = ((), (), s32[]{:S(2)}) async-start(), calls=%async_computation | async-start | bytes 245760
  113.7 52.1 %copy-start.5 = (f32[8,64]{1,0:T(8,128)S(1)}, f32[8,64]{1,0:T(8,128)}, u32[]{:S(2)}) copy-start(f32[8,64]{1,0:T(8,128)} %param.24) | copy-start | bytes 6148
  113.7 52.1 %copy-start.6 = (s32[128,1]{0,1:T(1,128)S(1)}, s32[128,1]{0,1:T(1,128)}, u32[]{:S(2)}) copy-start(s32[128,1]{0,1:T(1,128)} %param.23) | copy-start | bytes 1540
  113.7 52.2 %copy-start.4 = (f32[8,128]{1,0:T(8,128)S(1)}, f32[8,128]{1,0:T(8,128)}, u32[]{:S(2)}) copy-start(f32[8,128]{1,0:T(8,128)} %param.25) | copy-start | bytes 12292
  120.2 3.1 copy-start.1
  214.7 0.7 copy-start.2
  222.1 11.1 %copy-start.3 = (f32[32,256]{1,0:T(8,128)S(1)}, f32[32,256]{1,0:T(8,128)}, u32[]{:S(2)}) copy-start(f32[32,256]{1,0:T(8,128)} %param.15) | copy-start | bytes 98308
Sparse Core Ops, SparseCore 0:
  215.5 123.5 all-reduce.4
